TPU v7x, 512 devices: a whole 4x4x16 slice. The times are simulated.
512 devices in a mesh: ctx: 32 (over y_lo, z), fsdp: 16 (over x, y_hi, core).
Axes of the slice: x: 4, y: 4 (y_hi: 2, y_lo: 2; y = y_hi * 2 + y_lo), z: 16, core: 2. Of those that a mesh axis runs over, the one named last changes fastest.
Arguments:
- hidden_in: bfloat16 [16, 8192, 4096], P('fsdp', 'ctx'), may hold values from -40 to 40
- page_tokens: int32 [16, 16], P('fsdp'), may hold values from 1 to 1280, 8192 in all within a row
- grad_attn: bfloat16 [16, 8192, 128], P('fsdp', 'ctx'), may hold values from -6 to 6
- w_qkv: bfloat16 [4096, 384], P('fsdp'), may hold values from -1 to 1
Outputs:
- grad_hidden: bfloat16 [16, 8192, 4096], P('fsdp', 'ctx')
- grad_w_qkv: float32 [4096, 384], P('fsdp')
Inputs may be any that keep to these rules, and one draw needn't show every extreme that they name: `page_tokens`: each document's page lengths sum to 8192.
All inputs are finite; a program needn't handle non-finite values.
Results may differ from a plain program's by a relative error of at most 0.039.
Values may be sent and summed in bfloat16 or wider, within the bound.
A program may use at most 128 MiB of HBM per device.

v0:
```python
import jax
import jax.numpy as jnp
from jax import lax
from jax.sharding import PartitionSpec as P


def page_limits(page_row, positions, total_len):
    page_ends = jnp.cumsum(page_row)
    return jnp.min(
        jnp.where(page_ends[None, :] > positions[:, None], page_ends[None, :], total_len), axis=1
    )


def dot_rows(left, right):
    return lax.dot_general(
        left, right, (((1,), (1,)), ((), ())), preferred_element_type=jnp.float32
    )


def dot_cols(left, right):
    return lax.dot_general(
        left, right, (((0,), (0,)), ((), ())), preferred_element_type=jnp.float32
    )


def local(hidden_in, page_tokens, grad_attn, w_qkv):
    inputs_dev = hidden_in[0]
    grad_out = grad_attn[0]
    page_row = page_tokens[0]
    tok_rows = inputs_dev.shape[0]
    head_width = grad_out.shape[1]
    seq_len = tok_rows * lax.axis_size("ctx")
    score_scale = head_width ** (-0.5)
    weights_all = lax.all_gather(w_qkv, "fsdp", axis=0, tiled=True)
    projected = jnp.dot(inputs_dev, weights_all, preferred_element_type=jnp.float32)
    projected = projected.astype(jnp.bfloat16)
    queries = projected[:, :head_width]
    keys_own = projected[:, head_width : 2 * head_width]
    values_own = projected[:, 2 * head_width :]
    keys_all, values_all = (
        lax.all_gather(keys_own, "ctx", axis=0, tiled=True),
        lax.all_gather(values_own, "ctx", axis=0, tiled=True),
    )
    first_pos = lax.axis_index("ctx") * tok_rows
    positions = first_pos + jnp.arange(tok_rows, dtype=jnp.int32)
    limits = page_limits(page_row, positions, seq_len)
    key_pos = jnp.arange(seq_len, dtype=jnp.int32)
    visible = key_pos[None, :] < limits[:, None]
    scores = jnp.where(visible, dot_rows(queries, keys_all) * score_scale, -1e30)
    row_max = jnp.max(scores, axis=1, keepdims=True)
    log_total = row_max[:, 0] + jnp.log(jnp.sum(jnp.exp(scores - row_max), axis=1))
    probs_full = jnp.exp(scores - log_total[:, None])
    probs_half = probs_full.astype(jnp.bfloat16)
    attended = jnp.dot(probs_half, values_all, preferred_element_type=jnp.float32)
    out_dot = jnp.sum(grad_out.astype(jnp.float32) * attended, axis=1)
    dprob = dot_rows(grad_out, values_all)
    dscore = (probs_full * (dprob - out_dot[:, None]) * score_scale).astype(jnp.bfloat16)
    query_grad = jnp.dot(dscore, keys_all, preferred_element_type=jnp.float32)
    q_piece = lax.all_gather(queries.astype(jnp.float32), "ctx", axis=0, tiled=True).astype(
        jnp.bfloat16
    )
    grad_piece = lax.all_gather(grad_out.astype(jnp.float32), "ctx", axis=0, tiled=True).astype(
        jnp.bfloat16
    )
    total_piece = lax.all_gather(log_total, "ctx", axis=0, tiled=True)
    dot_piece = lax.all_gather(out_dot, "ctx", axis=0, tiled=True)
    piece_rows = q_piece.shape[0]
    piece_limits = page_limits(page_row, jnp.arange(piece_rows, dtype=jnp.int32), seq_len)
    seen = positions[None, :] < piece_limits[:, None]
    piece_scores = jnp.where(seen, dot_rows(q_piece, keys_own) * score_scale, -1e30)
    piece_probs = jnp.exp(piece_scores - total_piece[:, None])
    piece_half = piece_probs.astype(jnp.bfloat16)
    piece_dprob = dot_rows(grad_piece, values_own)
    piece_dscore = (piece_probs * (piece_dprob - dot_piece[:, None]) * score_scale).astype(
        jnp.bfloat16
    )
    key_grad = dot_cols(piece_dscore, q_piece)
    value_grad = dot_cols(piece_half, grad_piece)
    grad_qkv = jnp.concatenate([query_grad, key_grad, value_grad], axis=1).astype(jnp.bfloat16)
    grad_inputs = dot_rows(grad_qkv, weights_all)
    grad_inputs = grad_inputs.astype(jnp.bfloat16)[None]
    block_term = dot_cols(inputs_dev, grad_qkv).astype(jnp.bfloat16)
    block_sum = lax.psum_scatter(
        lax.optimization_barrier(block_term).astype(jnp.float32).astype(jnp.bfloat16),
        "fsdp",
        scatter_dimension=0,
        tiled=True,
    ).astype(jnp.float32)
    grad_weights = lax.psum(block_sum, "ctx")
    return (grad_inputs, grad_weights)


def solution(mesh):
    in_specs = (P("fsdp", "ctx", None), P("fsdp", None), P("fsdp", "ctx", None), P("fsdp", None))
    out_specs = (P("fsdp", "ctx", None), P("fsdp", None))
    return jax.shard_map(local, mesh=mesh, in_specs=in_specs, out_specs=out_specs, check_vma=False)
```

profile of v0, /device:TPU:8, one launch (start us, length us, event | category | flops | bytes accessed | tf_op | source)
XLA Modules:
  0.0 845.2 jit_solution(10110642753795459561)
XLA Ops:
  7.2 0.7 all-gather.8.cloned.1.call-update
  8.0 74.5 %all-gather.8.cloned.1.call-done = bf16[4096,384]{1,0:T(8,128)(2,1)} async-done(((bf16[256,384]{1,0:T(8,128)(2,1)}), bf16[4096,384]{1,0:T(8,128)(2,1)}) %all-gather.8.cloned.1.call-update) | async-done | bytes 3145744 | tf_op jit(solution)/shard_map/all_gather | solution.py:34
  82.5 3.1 fusion.25
  85.7 0.7 fusion.54
  86.4 0.0 all-gather.12.cloned.1.call-start
  86.4 0.7 all-gather.12.cloned.1.call-update
  87.1 0.5 all-gather.14.cloned.1.call-update
  87.7 0.7 copy.18
  88.5 0.0 reduce-scatter.2.cloned.1.call-start
  88.5 0.1 copy.17
  88.7 0.1 reduce
  88.8 0.1 select_reduce_fusion.1
  88.9 0.2 select_reduce_fusion
  89.1 129.8 %all-gather.10.cloned.1.call-done = bf16[8192,128]{1,0:T(8,128)(2,1)} async-done(((bf16[256,128]{1,0:T(8,128)(2,1)}), bf16[8192,128]{1,0:T(8,128)(2,1)}) %all-gather.10.cloned.1.call-update) | async-done | bytes 2097168 | tf_op jit(solution)/shard_map/all_gather | solution.py:41
  218.9 3.3 fusion.55
  222.2 1.3 exponential_reduce_fusion
  223.6 1.8 copy-done.1
  225.5 123.1 %all-gather.12.cloned.1.call-done = bf16[8192,128]{1,0:T(8,128)(2,1)} async-done(((bf16[256,128]{1,0:T(8,128)(2,1)}), bf16[8192,128]{1,0:T(8,128)(2,1)}) %all-gather.12.cloned.1.call-update) | async-done | bytes 2097168 | tf_op jit(solution)/shard_map/all_gather | solution.py:42
  348.6 5.7 fusion.36
  354.3 61.5 %all-gather.1 = f32[32,1,256]{2,1,0:T(1,128)S(1)} all-gather(f32[1,1,256]{2,1,0:T(1,128)S(1)} %bitcast.63), channel_id=1, replica_groups=mesh['ctx'=32,'fsdp'=16] {'ctx'}, dimensions={0}, use_global_device_ids=true | all-gather | bytes 33792 | tf_op jit(solution)/shard_map/all_gather | solution.py:66
  415.8 58.6 %all-gather = f32[32,1,256]{2,1,0:T(1,128)S(1)} all-gather(f32[1,1,256]{2,1,0:T(1,128)S(1)} %bitcast.62), channel_id=1, replica_groups=mesh['ctx'=32,'fsdp'=16] {'ctx'}, dimensions={0}, use_global_device_ids=true | all-gather | bytes 33792 | tf_op jit(solution)/shard_map/all_gather | solution.py:65
  474.4 3.6 all-gather.14.cloned.1.call-done
  478.1 7.7 fusion.9
  485.7 7.2 fusion.31
  492.9 109.0 %all-gather.16.cloned.1.call-done = bf16[8192,128]{0,1:T(8,128)(2,1)} async-done(((bf16[256,128]{0,1:T(8,128)(2,1)}), bf16[8192,128]{0,1:T(8,128)(2,1)}) %all-gather.16.cloned.1.call-update) | async-done | bytes 2097168 | tf_op jit(solution)/shard_map/all_gather | solution.py:62
  601.9 4.7 fusion.32
  606.6 7.1 fusion.35
  613.7 2.7 fusion.13
  616.4 4.5 fusion.14
  620.9 89.6 %reduce-scatter.2.cloned.1.call-done = bf16[256,384]{0,1:T(8,128)(2,1)} async-done(((bf16[4096,384]{0,1:T(8,128)(2,1)}), bf16[256,384]{0,1:T(8,128)(2,1)}) %reduce-scatter.2.cloned.1.call-update) | async-done | bytes 196624 | tf_op jit(solution)/shard_map/reduce_scatter | solution.py:83
  710.5 126.9 %all-reduce.1 = f32[256,384]{0,1:T(8,128)S(1)} all-reduce(bf16[256,384]{0,1:T(8,128)(2,1)} %reduce-scatter.2.cloned.1.call-done), channel_id=1, replica_groups=mesh['ctx'=32,'fsdp'=16] {'ctx'}, use_global_device_ids=true, to_apply=%region_7.8 | all-reduce | flops 98304 | bytes 589824 | tf_op jit(solution)/shard_map/psum | solution.py:89
  837.4 0.9 copy.21
  (19 shorter events, 0.3 us)
Async XLA Ops:
  7.2 75.3 %copy-start = (bf16[1,256,4096]{2,1,0:T(8,128)(2,1)S(1)}, bf16[1,256,4096]{2,1,0:T(8,128)(2,1)}, u32[]{:S(2)}) copy-start(bf16[1,256,4096]{2,1,0:T(8,128)(2,1)} %param.4) | copy-start | bytes 6291460
  7.2 80.5 %copy-start.3 = (bf16[1,256,128]{2,1,0:T(8,128)(2,1)S(1)}, bf16[1,256,128]{2,1,0:T(8,128)(2,1)}, u32[]{:S(2)}) copy-start(bf16[1,256,128]{2,1,0:T(8,128)(2,1)} %param.6) | copy-start | bytes 196612
  7.2 81.3 %copy-start.4 = (s32[1,16]{1,0:T(1,128)S(1)}, s32[1,16]{1,0:T(1,128)}, u32[]{:S(2)}) copy-start(s32[1,16]{1,0:T(1,128)} %param.5) | copy-start | bytes 196
  7.2 75.3 %all-gather.8.cloned.1.call-start = ((), (), s32[]{:S(2)}) async-start(), calls=%async_computation.1 | async-start | bytes 3342336 | tf_op jit(solution)/shard_map/all_gather | solution.py:34
  7.9 211.0 %all-gather.10.cloned.1.call-start = ((), (), s32[]{:S(2)}) async-start(), calls=%async_computation.2 | async-start | bytes 2162688 | tf_op jit(solution)/shard_map/all_gather | solution.py:41
  86.4 262.2 %all-gather.12.cloned.1.call-start = ((), (), s32[]{:S(2)}) async-start(), calls=%async_computation.3 | async-start | bytes 2162688 | tf_op jit(solution)/shard_map/all_gather | solution.py:42
  87.1 391.0 %all-gather.14.cloned.1.call-start = ((), (), s32[]{:S(2)}) async-start(), calls=%async_computation.4 | async-start | bytes 2162688 | tf_op jit(solution)/shard_map/all_gather | solution.py:59
  87.7 514.2 %all-gather.16.cloned.1.call-start = ((), (), s32[]{:S(2)}) async-start(), calls=%async_computation.5 | async-start | bytes 2162688 | tf_op jit(solution)/shard_map/all_gather | solution.py:62
  88.5 622.0 %reduce-scatter.2.cloned.1.call-start = ((), (), s32[]{:S(2)}) async-start(), calls=%async_computation.6 | async-start | bytes 3342336 | tf_op jit(solution)/shard_map/reduce_scatter | solution.py:83
  222.2 3.2 copy-start.1
  222.2 126.3 %copy-start.2 = (bf16[1,256,128]{1,2,0:T(8,128)(2,1)S(1)}, bf16[1,256,128]{1,2,0:T(8,128)(2,1)}, u32[]{:S(2)}) copy-start(bf16[1,256,128]{1,2,0:T(8,128)(2,1)} %copy.18) | copy-start | bytes 196612
Sparse Core Ops, SparseCore 0:
  11.3 71.1 all-gather.7
  86.5 132.4 all-gather.9
  221.6 126.9 all-gather.11
  351.1 126.9 all-gather.13
  479.9 121.9 all-gather.15
  616.5 93.9 reduce-scatter.1
where the time goes:
time: 846 us; the launch traced here: 845 us
  waiting for transfers between devices  532 us (63%)
  blocking collectives  247 us (29%)
  matrix products  45.9 us (5%)
  between operations  14.2 us (2%)
    all_gather x1, waiting for transfers between devices, local(): lax.all_gather(keys_own, 'ctx', axis=0, tiled=True)  130 us
    psum x1, blocking collectives, local(): grad_weights = lax.psum(block_sum, 'ctx')  127 us
    all_gather x1, waiting for transfers between devices, local(): lax.all_gather(values_own, 'ctx', axis=0, tiled=True)  123 us
    all_gather x1, waiting for transfers between devices, local(): lax.all_gather(grad_out.astype(jnp.float32), 'ctx', axis=0, tiled=True)  109 us
    reduce_scatter x1, waiting for transfers between devices, local(): lax.psum_scatter(lax.optimization_barrier(block_term).astype(jnp.float32)...  89.6 us
    all_gather x1, waiting for transfers between devices, local(): weights_all = lax.all_gather(w_qkv, 'fsdp', axis=0, tiled=True)  74.5 us
    all_gather x1, blocking collectives, local(): dot_piece = lax.all_gather(out_dot, 'ctx', axis=0, tiled=True)  61.5 us
    all_gather x1, blocking collectives, local(): total_piece = lax.all_gather(log_total, 'ctx', axis=0, tiled=True)  58.6 us
  transfers between devices with their start and end apart: 6, of which 6 were waited for; matrix products, arithmetic and copies ran while one was open for 4% of the time, Pallas kernels for 0%

commit v1 on v0

--- a/solution.py
+++ b/solution.py
@@ -2,6 +2,13 @@
 import jax.numpy as jnp
 from jax import lax
 from jax.sharding import PartitionSpec as P
+
+
+def exchange_gather(x, axis, dim):
+    count = lax.axis_size(axis)
+    shards = jnp.stack([x for _ in range(count)])
+    shards = lax.all_to_all(shards, axis, split_axis=0, concat_axis=0)
+    return jnp.concatenate(shards, axis=dim)
 
 
 def page_limits(page_row, positions, total_len):
@@ -31,7 +38,7 @@
     head_width = grad_out.shape[1]
     seq_len = tok_rows * lax.axis_size("ctx")
     score_scale = head_width ** (-0.5)
-    weights_all = lax.all_gather(w_qkv, "fsdp", axis=0, tiled=True)
+    weights_all = exchange_gather(w_qkv, "fsdp", 0)
     projected = jnp.dot(inputs_dev, weights_all, preferred_element_type=jnp.float32)
     projected = projected.astype(jnp.bfloat16)
     queries = projected[:, :head_width]

time: 846 us -> 819 us (0.968)
  waiting for transfers between devices: 532 us -> 458 us
  blocking collectives: 247 us -> 293 us
    all_gather x1 -> x0, waiting for transfers between devices: 74.5 us -> none  [local(): weights_all = lax.all_gather(w_qkv, 'fsdp', axis=0, tiled=True)]
    all_to_all x0 -> x1, blocking collectives: none -> 46.4 us  [exchange_gather(): shards = lax.all_to_all(shards, axis, split_axis=0, concat_axis=0)]
  transfers between devices with their start and end apart: 6 -> 5, of which waited for: 6 -> 5; matrix products, arithmetic and copies ran while one was open for 4% -> 4% of each run, Pallas kernels for 0% -> 0%
where the time goes in v1:
time: 819 us; the launch traced here: 818 us
  waiting for transfers between devices  458 us (56%)
  blocking collectives  293 us (36%)
  matrix products  44.1 us (5%)
  between operations  13.9 us (2%)
    all_gather x1, waiting for transfers between devices, local(): lax.all_gather(keys_own, 'ctx', axis=0, tiled=True)  131 us
    psum x1, blocking collectives, local(): grad_weights = lax.psum(block_sum, 'ctx')  127 us
    all_gather x1, waiting for transfers between devices, local(): lax.all_gather(values_own, 'ctx', axis=0, tiled=True)  123 us
    all_gather x1, waiting for transfers between devices, local(): lax.all_gather(grad_out.astype(jnp.float32), 'ctx', axis=0, tiled=True)  109 us
    reduce_scatter x1, waiting for transfers between devices, local(): lax.psum_scatter(lax.optimization_barrier(block_term).astype(jnp.float32)...  89.8 us
    all_gather x1, blocking collectives, local(): dot_piece = lax.all_gather(out_dot, 'ctx', axis=0, tiled=True)  61.5 us
    all_gather x1, blocking collectives, local(): total_piece = lax.all_gather(log_total, 'ctx', axis=0, tiled=True)  58.6 us
    all_to_all x1, blocking collectives, exchange_gather(): shards = lax.all_to_all(shards, axis, split_axis=0, concat_axis=0)  46.4 us
  transfers between devices with their start and end apart: 5, of which 5 were waited for; matrix products, arithmetic and copies ran while one was open for 4% of the time, Pallas kernels for 0%

profile of v1, /device:TPU:8, one launch (start us, length us, event | category | flops | bytes accessed | tf_op | source)
XLA Modules:
  0.0 818.5 jit_solution(14436294717102385232)
XLA Ops:
  7.2 1.5 stack.2
  8.7 46.4 %all_to_all.5 = bf16[16,256,384]{2,1,0:T(8,128)(2,1)S(1)} all-to-all(bf16[16,256,384]{2,1,0:T(8,128)(2,1)S(1)} %stack.2), channel_id=1, replica_groups=mesh['ctx'=32,'fsdp'=16] {'fsdp'}, dimensions={0} | all-to-all | bytes 6291456 | tf_op jit(solution)/shard_map/all_to_all | solution.py:10
  55.1 1.7 copy-done.2
  56.8 1.3 fusion.25
  58.1 0.7 fusion.54
  58.8 0.7 all-gather.9.cloned.1.call-update
  59.6 0.7 all-gather.11.cloned.1.call-update
  60.3 0.7 copy.18
  61.1 0.0 reduce-scatter.2.cloned.1.call-start
  61.1 0.1 copy.17
  61.2 0.1 reduce
  61.4 0.1 select_reduce_fusion.1
  61.5 0.2 select_reduce_fusion
  61.7 130.7 %all-gather.7.cloned.1.call-done = bf16[8192,128]{1,0:T(8,128)(2,1)} async-done(((bf16[256,128]{1,0:T(8,128)(2,1)}), bf16[8192,128]{1,0:T(8,128)(2,1)}) %all-gather.7.cloned.1.call-update) | async-done | bytes 2097168 | tf_op jit(solution)/shard_map/all_gather | solution.py:48
  192.4 3.3 fusion.55
  195.7 1.3 exponential_reduce_fusion
  197.0 1.8 copy-done.1
  198.9 123.1 %all-gather.9.cloned.1.call-done = bf16[8192,128]{1,0:T(8,128)(2,1)} async-done(((bf16[256,128]{1,0:T(8,128)(2,1)}), bf16[8192,128]{1,0:T(8,128)(2,1)}) %all-gather.9.cloned.1.call-update) | async-done | bytes 2097168 | tf_op jit(solution)/shard_map/all_gather | solution.py:49
  322.0 5.7 fusion.36
  327.7 61.5 %all-gather.1 = f32[32,1,256]{2,1,0:T(1,128)S(1)} all-gather(f32[1,1,256]{2,1,0:T(1,128)S(1)} %bitcast.66), channel_id=1, replica_groups=mesh['ctx'=32,'fsdp'=16] {'ctx'}, dimensions={0}, use_global_device_ids=true | all-gather | bytes 33792 | tf_op jit(solution)/shard_map/all_gather | solution.py:73
  389.2 58.6 %all-gather = f32[32,1,256]{2,1,0:T(1,128)S(1)} all-gather(f32[1,1,256]{2,1,0:T(1,128)S(1)} %bitcast.65), channel_id=1, replica_groups=mesh['ctx'=32,'fsdp'=16] {'ctx'}, dimensions={0}, use_global_device_ids=true | all-gather | bytes 33792 | tf_op jit(solution)/shard_map/all_gather | solution.py:72
  447.8 3.8 all-gather.11.cloned.1.call-done
  451.6 7.7 fusion.9
  459.3 7.2 fusion.31
  466.4 108.9 %all-gather.13.cloned.1.call-done = bf16[8192,128]{0,1:T(8,128)(2,1)} async-done(((bf16[256,128]{0,1:T(8,128)(2,1)}), bf16[8192,128]{0,1:T(8,128)(2,1)}) %all-gather.13.cloned.1.call-update) | async-done | bytes 2097168 | tf_op jit(solution)/shard_map/all_gather | solution.py:69
  575.3 4.7 fusion.32
  580.0 7.1 fusion.35
  587.1 2.7 fusion.13
  589.8 4.5 fusion.14
  594.3 89.8 %reduce-scatter.2.cloned.1.call-done = bf16[256,384]{0,1:T(8,128)(2,1)} async-done(((bf16[4096,384]{0,1:T(8,128)(2,1)}), bf16[256,384]{0,1:T(8,128)(2,1)}) %reduce-scatter.2.cloned.1.call-update) | async-done | bytes 196624 | tf_op jit(solution)/shard_map/reduce_scatter | solution.py:90
  684.1 126.9 %all-reduce.1 = f32[256,384]{0,1:T(8,128)S(1)} all-reduce(bf16[256,384]{0,1:T(8,128)(2,1)} %reduce-scatter.2.cloned.1.call-done), channel_id=1, replica_groups=mesh['ctx'=32,'fsdp'=16] {'ctx'}, use_global_device_ids=true, to_apply=%region_7.8 | all-reduce | flops 98304 | bytes 589824 | tf_op jit(solution)/shard_map/psum | solution.py:96
  811.0 0.9 copy.21
  (20 shorter events, 0.3 us)
Async XLA Ops:
  7.2 49.6 %copy-start = (bf16[1,256,4096]{2,1,0:T(8,128)(2,1)S(1)}, bf16[1,256,4096]{2,1,0:T(8,128)(2,1)}, u32[]{:S(2)}) copy-start(bf16[1,256,4096]{2,1,0:T(8,128)(2,1)} %param.4) | copy-start | bytes 6291460
  7.2 185.2 %all-gather.7.cloned.1.call-start = ((), (), s32[]{:S(2)}) async-start(), calls=%async_computation.2 | async-start | bytes 2162688 | tf_op jit(solution)/shard_map/all_gather | solution.py:48
  55.1 1.7 copy-start.2
  55.1 5.2 copy-start.4
  55.1 6.0 copy-start.5
  58.8 263.2 %all-gather.9.cloned.1.call-start = ((), (), s32[]{:S(2)}) async-start(), calls=%async_computation.3 | async-start | bytes 2162688 | tf_op jit(solution)/shard_map/all_gather | solution.py:49
  59.5 392.1 %all-gather.11.cloned.1.call-start = ((), (), s32[]{:S(2)}) async-start(), calls=%async_computation.4 | async-start | bytes 2162688 | tf_op jit(solution)/shard_map/all_gather | solution.py:66
  60.2 515.1 %all-gather.13.cloned.1.call-start = ((), (), s32[]{:S(2)}) async-start(), calls=%async_computation.5 | async-start | bytes 2162688 | tf_op jit(solution)/shard_map/all_gather | solution.py:69
  61.1 623.0 %reduce-scatter.2.cloned.1.call-start = ((), (), s32[]{:S(2)}) async-start(), calls=%async_computation.6 | async-start | bytes 3342336 | tf_op jit(solution)/shard_map/reduce_scatter | solution.py:90
  195.7 3.2 copy-start.1
  195.7 126.3 %copy-start.3 = (bf16[1,256,128]{1,2,0:T(8,128)(2,1)S(1)}, bf16[1,256,128]{1,2,0:T(8,128)(2,1)}, u32[]{:S(2)}) copy-start(bf16[1,256,128]{1,2,0:T(8,128)(2,1)} %copy.18) | copy-start | bytes 196612
Sparse Core Ops, SparseCore 0:
  58.9 133.4 all-gather.6
  195.0 126.9 all-gather.8
  324.7 126.9 all-gather.10
  453.5 121.7 all-gather.12
  589.9 94.1 reduce-scatter.1
